TPU v7x, 32 devices: a whole 2x2x4 slice. The times are simulated.
32 devices in a mesh: depth: 4 (over y, core), tile: 8 (over z, x).
Axes of the slice: x: 2, y: 2, z: 4, core: 2. Of those that a mesh axis runs over, the one named last changes fastest.
Arguments:
- fields: float32 [2, 128, 128, 1024], P(None, 'depth', 'tile'), may hold values from -6 to 6
- colour_palette: float32 [3, 16], replicated, may hold values from 0.05 to 1
- opacity_palette: float32 [16], replicated, may hold values from 0.2 to 3
- tf_index: int32 [256], replicated, may hold values from 0 to 15
Outputs:
- image: float32 [4, 128, 1024], P(None, 'tile', 'depth')
All inputs are finite; a program needn't handle non-finite values.
Results may differ from a plain program's by a relative error of at most 0.0003.
Values sent between devices are 32-bit elements; how exact they have to be, the bound alone decides.
No kernel may reach another device: no remote copies, remote signals or barrier semaphores. Data moves between devices by JAX's collectives and lax.ppermute only.
A program may use at most 64 MiB of HBM per device.

v0:
```python
import jax
import jax.numpy as jnp
import numpy as np
from jax import lax
from jax.sharding import PartitionSpec as P

taps_offset = np.arange(-4.0, 5.0)
gauss_bell = np.exp(-(taps_offset**2) / 8.0)
smooth_taps = tuple((float(weight) for weight in gauss_bell / np.sqrt(np.sum(gauss_bell**2))))
slope_raw = taps_offset * gauss_bell
slope_taps = tuple((float(weight) for weight in slope_raw / np.sqrt(np.sum(slope_raw**2))))


def extended(cells, sides, width):
    for axis, dim in sides:
        count = lax.axis_size(axis)
        ends = count - 1
        head = lax.slice_in_dim(cells, 0, width, axis=dim)
        tail = lax.slice_in_dim(cells, cells.shape[dim] - width, cells.shape[dim], axis=dim)
        cells = jnp.concatenate(
            [
                lax.ppermute(tail, axis, [(i, (i + 1) % count) for i in range(ends)]),
                cells,
                lax.ppermute(head, axis, [((i + 1) % count, i) for i in range(ends)]),
            ],
            axis=dim,
        )
    return cells


def swapped(value, axis, apart):
    mask = 2**apart
    pairs = [(source, source ^ mask) for source in range(lax.axis_size(axis))]
    return lax.ppermute(value, axis, pairs)


def filter_axis(field, taps, axis):
    count = field.shape[axis] - (len(taps) - 1)
    total = taps[0] * lax.slice_in_dim(field, 0, count, axis=axis)
    for offset in range(1, len(taps)):
        total = total + taps[offset] * lax.slice_in_dim(field, offset, offset + count, axis=axis)
    return total


def smooth_three(field, first):
    for axis in range(first, first + 3):
        field = filter_axis(field, smooth_taps, axis)
    return field


def slopes(smooth_a):
    core = smooth_a[4:-4, 4:-4, 4:-4]
    grad_z = filter_axis(smooth_a[:, 4:-4, 4:-4], slope_taps, 0)
    grad_x = filter_axis(smooth_a[4:-4, :, 4:-4], slope_taps, 1)
    grad_y = filter_axis(smooth_a[4:-4, 4:-4, :], slope_taps, 2)
    return (core, grad_z, grad_x, grad_y)


def shade_cells(smooth_a, smooth_b, grad_z, grad_x, grad_y, table, depth_total):
    bins = table.shape[1]
    slab_cells, strip_rows, column_count = smooth_a.shape
    level = (bins - 1) * jax.nn.sigmoid(1.5 * smooth_a)
    centres = jnp.arange(bins, dtype=jnp.float32)

    def one_plane(plane):
        flat = plane.reshape(1, strip_rows * column_count)
        hat_weights = jnp.maximum(0.0, 1.0 - jnp.abs(flat - centres[:, None]))
        mixed = jnp.dot(table, hat_weights, precision=lax.Precision.HIGHEST)
        return mixed.reshape(4, strip_rows, column_count)

    looked = jnp.moveaxis(lax.map(one_plane, level), 1, 0)
    facing = jnp.abs(0.26726 * grad_z + 0.53452 * grad_x + 0.80178 * grad_y)
    length = jnp.sqrt(jnp.maximum(grad_z * grad_z + grad_x * grad_x + grad_y * grad_y, 0.1))
    shade = 0.3 + 0.7 * facing / length
    optical = 1.5 * (2.0 / depth_total) * looked[3] * jax.nn.sigmoid(2.0 * smooth_b)
    depth_ids = jnp.arange(slab_cells, dtype=jnp.int32)
    strict_lower = (depth_ids[:, None] > depth_ids[None, :]).astype(jnp.float32)
    flat_optical = optical.reshape(slab_cells, strip_rows * column_count)
    before = jnp.dot(strict_lower, flat_optical, precision=lax.Precision.HIGHEST).reshape(
        optical.shape
    )
    ones_row = jnp.ones((1, slab_cells), jnp.float32)
    total = jnp.dot(ones_row, flat_optical, precision=lax.Precision.HIGHEST).reshape(
        strip_rows, column_count
    )
    weight = jnp.exp(-before) * -jnp.expm1(-optical)
    colour = jnp.sum(weight[None] * looked[:3] * shade[None], axis=1)
    return jnp.concatenate([colour, jnp.exp(-total)[None]], axis=0)


def blend_over(front, back):
    colour = front[:3] + front[3:4] * back[:3]
    return jnp.concatenate([colour, front[3:4] * back[3:4]], axis=0)


def local(fields, colour_palette, opacity_palette, tf_index):
    palette_size = colour_palette.shape[1]
    one_hot = (tf_index[None, :] == jnp.arange(palette_size, dtype=jnp.int32)[:, None]).astype(
        jnp.float32
    )
    table = jnp.concatenate(
        [
            jnp.dot(colour_palette, one_hot, precision=lax.Precision.HIGHEST),
            jnp.dot(opacity_palette[None], one_hot, precision=lax.Precision.HIGHEST),
        ],
        axis=0,
    )
    depth_count = lax.axis_size("depth")
    slab_cells = fields.shape[1]
    strip_rows = fields.shape[2]
    depth_total = slab_cells * depth_count
    wide_first = extended(fields[0], (("depth", 0), ("tile", 1)), 8)
    wide_first = jnp.pad(wide_first, ((0, 0), (0, 0), (8, 8)))
    wide_second = extended(fields[1], (("depth", 0), ("tile", 1)), 4)
    wide_second = jnp.pad(wide_second, ((0, 0), (0, 0), (4, 4)))
    smooth_a = smooth_three(wide_first, 0)
    smooth_b = smooth_three(wide_second, 0)
    depth_pos = (
        lax.axis_index("depth") * slab_cells - 4 + jnp.arange(slab_cells + 8, dtype=jnp.int32)
    )
    depth_ok = (depth_pos >= 0) & (depth_pos < depth_total)
    row_total = strip_rows * lax.axis_size("tile")
    row_pos = lax.axis_index("tile") * strip_rows - 4 + jnp.arange(strip_rows + 8, dtype=jnp.int32)
    row_ok = (row_pos >= 0) & (row_pos < row_total)
    column_count = fields.shape[3]
    column_pos = jnp.arange(column_count + 8, dtype=jnp.int32) - 4
    column_ok = (column_pos >= 0) & (column_pos < column_count)
    inside = depth_ok[:, None, None] & row_ok[None, :, None] & column_ok[None, None, :]
    smooth_a = jnp.where(inside, smooth_a, jnp.float32(0.0))
    core, grad_z, grad_x, grad_y = slopes(smooth_a)
    partial_value = shade_cells(core, smooth_b, grad_z, grad_x, grad_y, table, depth_total)
    rows, columns = (partial_value.shape[1], partial_value.shape[2])
    own_columns = columns // depth_count
    levels = depth_count.bit_length() - 1
    depth_index = lax.axis_index("depth")
    current = partial_value.reshape((4, rows) + (2,) * levels + (own_columns,))
    for bit in range(levels):
        axis = 2 + (levels - 1 - bit)
        my_bit = depth_index // 2**bit % 2
        keeping = lax.dynamic_index_in_dim(current, my_bit, axis, keepdims=False)
        sending = lax.dynamic_index_in_dim(current, 1 - my_bit, axis, keepdims=False)
        partner = swapped(sending, "depth", bit)
        mine_front = my_bit == 0
        current = jnp.where(mine_front, blend_over(keeping, partner), blend_over(partner, keeping))
    return current


def solution(mesh):
    placed = (P(None, "depth", "tile", None), P(), P(), P())
    return jax.shard_map(
        local, mesh=mesh, in_specs=placed, out_specs=P(None, "tile", "depth"), check_vma=False
    )
```

profile of v0, /device:TPU:0, one launch (start us, length us, event | category | flops | bytes accessed | tf_op | source)
XLA Modules:
  0.0 996.2 jit_solution(13898019109590667645)
XLA Ops:
  41.6 48.5 %collective-permute-done.6 = f32[40,4,1024]{2,0,1:T(8,128)} collective-permute-done((f32[40,4,1024]{2,0,1:T(8,128)}, f32[40,4,1024]{2,0,1:T(8,128)}, u32[]{:S(2)}, u32[]{:S(2)}) %collective-permute-start.6) | collective-permute-done | bytes 655392 | tf_op jit(solution)/shard_map/ppermute | solution.py:22
  101.7 22.2 %collective-permute-done.2 = f32[48,8,1024]{2,0,1:T(8,128)S(1)} collective-permute-done((f32[48,8,1024]{2,0,1:T(8,128)}, f32[48,8,1024]{2,0,1:T(8,128)S(1)}, u32[]{:S(2)}, u32[]{:S(2)}) %collective-permute-start.2) | collective-permute-done | bytes 1572896 | tf_op jit(solution)/shard_map/ppermute | solution.py:22
  164.6 17.7 %multiply_add_fusion = f32[32,16,1024]{2,0,1:T(8,128)} fusion(f32[40,24,1032]{2,0,1:T(8,128)S(1)} %fusion.23), kind=kLoop, calls=%fused_computation.195 | loop fusion | flops 33554432 | bytes 54525952 | tf_op jit(solution)/shard_map/add | solution.py:74
  184.6 792.7 %while.11 = (s32[]{:T(128)}, f32[32,4,16,1024]{3,0,2,1:T(8,128)}, f32[32,16,1024]{2,0,1:T(8,128)}, f32[4,256]{1,0:T(4,128)S(1)}, s32[]{:T(128)}, /*index=5*/s32[]{:T(128)}) while((s32[]{:T(128)}, f32[32,4,16,1024]{3,0,2,1:T(8,128)}, f32[32,16,1024]{2,0,1:T(8,128)}, f32[4,256]{1,0:T(4,128)S(1)}, s32[]{:T(128)}, ...), condition=%wide.region_1.2_spmd.clone, body=%wide.region_0.1_spmd.clone.sunk | while | flops 218103808 | bytes 1511509 | solution.py:71
  185.6 17.2 %convolution_bitcast_fusion.3 = f32[4,16384]{1,0:T(4,128)S(1)} fusion(f32[4,256]{1,0:T(4,128)S(1)} %get-tuple-element.125, f32[16384]{0:T(1024)S(1)} %bitcast.113), kind=kOutput, calls=%fused_computation.1.clone.1 | convolution fusion | flops 218103808 | bytes 331776 | tf_op jit(solution)/shard_map/while/body/eval_jaxpr/dot_general | solution.py:68
  210.4 17.2 %convolution_bitcast_fusion.3 = f32[4,16384]{1,0:T(4,128)S(1)} fusion(f32[4,256]{1,0:T(4,128)S(1)} %get-tuple-element.125, f32[16384]{0:T(1024)S(1)} %bitcast.113), kind=kOutput, calls=%fused_computation.1.clone.1 | convolution fusion | flops 218103808 | bytes 331776 | tf_op jit(solution)/shard_map/while/body/eval_jaxpr/dot_general | solution.py:68
  235.2 17.2 %convolution_bitcast_fusion.3 = f32[4,16384]{1,0:T(4,128)S(1)} fusion(f32[4,256]{1,0:T(4,128)S(1)} %get-tuple-element.125, f32[16384]{0:T(1024)S(1)} %bitcast.113), kind=kOutput, calls=%fused_computation.1.clone.1 | convolution fusion | flops 218103808 | bytes 331776 | tf_op jit(solution)/shard_map/while/body/eval_jaxpr/dot_general | solution.py:68
  260.0 17.2 %convolution_bitcast_fusion.3 = f32[4,16384]{1,0:T(4,128)S(1)} fusion(f32[4,256]{1,0:T(4,128)S(1)} %get-tuple-element.125, f32[16384]{0:T(1024)S(1)} %bitcast.113), kind=kOutput, calls=%fused_computation.1.clone.1 | convolution fusion | flops 218103808 | bytes 331776 | tf_op jit(solution)/shard_map/while/body/eval_jaxpr/dot_general | solution.py:68
  284.8 17.2 %convolution_bitcast_fusion.3 = f32[4,16384]{1,0:T(4,128)S(1)} fusion(f32[4,256]{1,0:T(4,128)S(1)} %get-tuple-element.125, f32[16384]{0:T(1024)S(1)} %bitcast.113), kind=kOutput, calls=%fused_computation.1.clone.1 | convolution fusion | flops 218103808 | bytes 331776 | tf_op jit(solution)/shard_map/while/body/eval_jaxpr/dot_general | solution.py:68
  334.3 17.2 %convolution_bitcast_fusion.3 = f32[4,16384]{1,0:T(4,128)S(1)} fusion(f32[4,256]{1,0:T(4,128)S(1)} %get-tuple-element.125, f32[16384]{0:T(1024)S(1)} %bitcast.113), kind=kOutput, calls=%fused_computation.1.clone.1 | convolution fusion | flops 218103808 | bytes 331776 | tf_op jit(solution)/shard_map/while/body/eval_jaxpr/dot_general | solution.py:68
  359.1 17.2 %convolution_bitcast_fusion.3 = f32[4,16384]{1,0:T(4,128)S(1)} fusion(f32[4,256]{1,0:T(4,128)S(1)} %get-tuple-element.125, f32[16384]{0:T(1024)S(1)} %bitcast.113), kind=kOutput, calls=%fused_computation.1.clone.1 | convolution fusion | flops 218103808 | bytes 331776 | tf_op jit(solution)/shard_map/while/body/eval_jaxpr/dot_general | solution.py:68
  408.6 17.2 %convolution_bitcast_fusion.3 = f32[4,16384]{1,0:T(4,128)S(1)} fusion(f32[4,256]{1,0:T(4,128)S(1)} %get-tuple-element.125, f32[16384]{0:T(1024)S(1)} %bitcast.113), kind=kOutput, calls=%fused_computation.1.clone.1 | convolution fusion | flops 218103808 | bytes 331776 | tf_op jit(solution)/shard_map/while/body/eval_jaxpr/dot_general | solution.py:68
  433.3 17.2 %convolution_bitcast_fusion.3 = f32[4,16384]{1,0:T(4,128)S(1)} fusion(f32[4,256]{1,0:T(4,128)S(1)} %get-tuple-element.125, f32[16384]{0:T(1024)S(1)} %bitcast.113), kind=kOutput, calls=%fused_computation.1.clone.1 | convolution fusion | flops 218103808 | bytes 331776 | tf_op jit(solution)/shard_map/while/body/eval_jaxpr/dot_general | solution.py:68
  458.1 17.2 %convolution_bitcast_fusion.3 = f32[4,16384]{1,0:T(4,128)S(1)} fusion(f32[4,256]{1,0:T(4,128)S(1)} %get-tuple-element.125, f32[16384]{0:T(1024)S(1)} %bitcast.113), kind=kOutput, calls=%fused_computation.1.clone.1 | convolution fusion | flops 218103808 | bytes 331776 | tf_op jit(solution)/shard_map/while/body/eval_jaxpr/dot_general | solution.py:68
  482.8 17.2 %convolution_bitcast_fusion.3 = f32[4,16384]{1,0:T(4,128)S(1)} fusion(f32[4,256]{1,0:T(4,128)S(1)} %get-tuple-element.125, f32[16384]{0:T(1024)S(1)} %bitcast.113), kind=kOutput, calls=%fused_computation.1.clone.1 | convolution fusion | flops 218103808 | bytes 331776 | tf_op jit(solution)/shard_map/while/body/eval_jaxpr/dot_general | solution.py:68
  507.5 17.2 %convolution_bitcast_fusion.3 = f32[4,16384]{1,0:T(4,128)S(1)} fusion(f32[4,256]{1,0:T(4,128)S(1)} %get-tuple-element.125, f32[16384]{0:T(1024)S(1)} %bitcast.113), kind=kOutput, calls=%fused_computation.1.clone.1 | convolution fusion | flops 218103808 | bytes 331776 | tf_op jit(solution)/shard_map/while/body/eval_jaxpr/dot_general | solution.py:68
  532.2 17.2 %convolution_bitcast_fusion.3 = f32[4,16384]{1,0:T(4,128)S(1)} fusion(f32[4,256]{1,0:T(4,128)S(1)} %get-tuple-element.125, f32[16384]{0:T(1024)S(1)} %bitcast.113), kind=kOutput, calls=%fused_computation.1.clone.1 | convolution fusion | flops 218103808 | bytes 331776 | tf_op jit(solution)/shard_map/while/body/eval_jaxpr/dot_general | solution.py:68
  557.0 17.2 %convolution_bitcast_fusion.3 = f32[4,16384]{1,0:T(4,128)S(1)} fusion(f32[4,256]{1,0:T(4,128)S(1)} %get-tuple-element.125, f32[16384]{0:T(1024)S(1)} %bitcast.113), kind=kOutput, calls=%fused_computation.1.clone.1 | convolution fusion | flops 218103808 | bytes 331776 | tf_op jit(solution)/shard_map/while/body/eval_jaxpr/dot_general | solution.py:68
  581.7 17.2 %convolution_bitcast_fusion.3 = f32[4,16384]{1,0:T(4,128)S(1)} fusion(f32[4,256]{1,0:T(4,128)S(1)} %get-tuple-element.125, f32[16384]{0:T(1024)S(1)} %bitcast.113), kind=kOutput, calls=%fused_computation.1.clone.1 | convolution fusion | flops 218103808 | bytes 331776 | tf_op jit(solution)/shard_map/while/body/eval_jaxpr/dot_general | solution.py:68
  606.5 17.2 %convolution_bitcast_fusion.3 = f32[4,16384]{1,0:T(4,128)S(1)} fusion(f32[4,256]{1,0:T(4,128)S(1)} %get-tuple-element.125, f32[16384]{0:T(1024)S(1)} %bitcast.113), kind=kOutput, calls=%fused_computation.1.clone.1 | convolution fusion | flops 218103808 | bytes 331776 | tf_op jit(solution)/shard_map/while/body/eval_jaxpr/dot_general | solution.py:68
  631.4 17.2 %convolution_bitcast_fusion.3 = f32[4,16384]{1,0:T(4,128)S(1)} fusion(f32[4,256]{1,0:T(4,128)S(1)} %get-tuple-element.125, f32[16384]{0:T(1024)S(1)} %bitcast.113), kind=kOutput, calls=%fused_computation.1.clone.1 | convolution fusion | flops 218103808 | bytes 331776 | tf_op jit(solution)/shard_map/while/body/eval_jaxpr/dot_general | solution.py:68
  656.2 17.2 %convolution_bitcast_fusion.3 = f32[4,16384]{1,0:T(4,128)S(1)} fusion(f32[4,256]{1,0:T(4,128)S(1)} %get-tuple-element.125, f32[16384]{0:T(1024)S(1)} %bitcast.113), kind=kOutput, calls=%fused_computation.1.clone.1 | convolution fusion | flops 218103808 | bytes 331776 | tf_op jit(solution)/shard_map/while/body/eval_jaxpr/dot_general | solution.py:68
  705.8 17.2 %convolution_bitcast_fusion.3 = f32[4,16384]{1,0:T(4,128)S(1)} fusion(f32[4,256]{1,0:T(4,128)S(1)} %get-tuple-element.125, f32[16384]{0:T(1024)S(1)} %bitcast.113), kind=kOutput, calls=%fused_computation.1.clone.1 | convolution fusion | flops 218103808 | bytes 331776 | tf_op jit(solution)/shard_map/while/body/eval_jaxpr/dot_general | solution.py:68
  730.7 17.2 %convolution_bitcast_fusion.3 = f32[4,16384]{1,0:T(4,128)S(1)} fusion(f32[4,256]{1,0:T(4,128)S(1)} %get-tuple-element.125, f32[16384]{0:T(1024)S(1)} %bitcast.113), kind=kOutput, calls=%fused_computation.1.clone.1 | convolution fusion | flops 218103808 | bytes 331776 | tf_op jit(solution)/shard_map/while/body/eval_jaxpr/dot_general | solution.py:68
  755.5 17.2 %convolution_bitcast_fusion.3 = f32[4,16384]{1,0:T(4,128)S(1)} fusion(f32[4,256]{1,0:T(4,128)S(1)} %get-tuple-element.125, f32[16384]{0:T(1024)S(1)} %bitcast.113), kind=kOutput, calls=%fused_computation.1.clone.1 | convolution fusion | flops 218103808 | bytes 331776 | tf_op jit(solution)/shard_map/while/body/eval_jaxpr/dot_general | solution.py:68
  780.3 17.2 %convolution_bitcast_fusion.3 = f32[4,16384]{1,0:T(4,128)S(1)} fusion(f32[4,256]{1,0:T(4,128)S(1)} %get-tuple-element.125, f32[16384]{0:T(1024)S(1)} %bitcast.113), kind=kOutput, calls=%fused_computation.1.clone.1 | convolution fusion | flops 218103808 | bytes 331776 | tf_op jit(solution)/shard_map/while/body/eval_jaxpr/dot_general | solution.py:68
  805.1 17.2 %convolution_bitcast_fusion.3 = f32[4,16384]{1,0:T(4,128)S(1)} fusion(f32[4,256]{1,0:T(4,128)S(1)} %get-tuple-element.125, f32[16384]{0:T(1024)S(1)} %bitcast.113), kind=kOutput, calls=%fused_computation.1.clone.1 | convolution fusion | flops 218103808 | bytes 331776 | tf_op jit(solution)/shard_map/while/body/eval_jaxpr/dot_general | solution.py:68
  854.6 17.2 %convolution_bitcast_fusion.3 = f32[4,16384]{1,0:T(4,128)S(1)} fusion(f32[4,256]{1,0:T(4,128)S(1)} %get-tuple-element.125, f32[16384]{0:T(1024)S(1)} %bitcast.113), kind=kOutput, calls=%fused_computation.1.clone.1 | convolution fusion | flops 218103808 | bytes 331776 | tf_op jit(solution)/shard_map/while/body/eval_jaxpr/dot_general | solution.py:68
  879.3 17.2 %convolution_bitcast_fusion.3 = f32[4,16384]{1,0:T(4,128)S(1)} fusion(f32[4,256]{1,0:T(4,128)S(1)} %get-tuple-element.125, f32[16384]{0:T(1024)S(1)} %bitcast.113), kind=kOutput, calls=%fused_computation.1.clone.1 | convolution fusion | flops 218103808 | bytes 331776 | tf_op jit(solution)/shard_map/while/body/eval_jaxpr/dot_general | solution.py:68
  904.1 17.2 %convolution_bitcast_fusion.3 = f32[4,16384]{1,0:T(4,128)S(1)} fusion(f32[4,256]{1,0:T(4,128)S(1)} %get-tuple-element.125, f32[16384]{0:T(1024)S(1)} %bitcast.113), kind=kOutput, calls=%fused_computation.1.clone.1 | convolution fusion | flops 218103808 | bytes 331776 | tf_op jit(solution)/shard_map/while/body/eval_jaxpr/dot_general | solution.py:68
  928.9 17.2 %convolution_bitcast_fusion.3 = f32[4,16384]{1,0:T(4,128)S(1)} fusion(f32[4,256]{1,0:T(4,128)S(1)} %get-tuple-element.125, f32[16384]{0:T(1024)S(1)} %bitcast.113), kind=kOutput, calls=%fused_computation.1.clone.1 | convolution fusion | flops 218103808 | bytes 331776 | tf_op jit(solution)/shard_map/while/body/eval_jaxpr/dot_general | solution.py:68
  953.6 17.2 %convolution_bitcast_fusion.3 = f32[4,16384]{1,0:T(4,128)S(1)} fusion(f32[4,256]{1,0:T(4,128)S(1)} %get-tuple-element.125, f32[16384]{0:T(1024)S(1)} %bitcast.113), kind=kOutput, calls=%fused_computation.1.clone.1 | convolution fusion | flops 218103808 | bytes 331776 | tf_op jit(solution)/shard_map/while/body/eval_jaxpr/dot_general | solution.py:68
  (195 shorter events, 426.0 us)
Async XLA Ops:
  0.0 19.2 %copy-start = (f32[3,16]{1,0:T(4,128)S(1)}, f32[3,16]{1,0:T(4,128)}, u32[]{:S(2)}) copy-start(f32[3,16]{1,0:T(4,128)} %param.7) | copy-start | bytes 580
  2.0 18.8 %collective-permute-start.5 = (f32[4,16,1024]{2,0,1:T(4,128)}, f32[4,16,1024]{2,0,1:T(4,128)S(1)}, u32[]{:S(2)}, u32[]{:S(2)}) collective-permute-start(f32[4,16,1024]{2,0,1:T(4,128)} %bitcast.94), channel_id=1, source_target_pairs={{8,0},{16,8},{24,16},{9,1},{17,9},{25,17},{10,2},{18,10},{26,18},{... | collective-permute-start | bytes 786440 | tf_op jit(solution)/shard_map/ppermute | solution.py:24
  3.2 14.1 %copy-start.8 = (f32[2,32,16,1024]{3,2,1,0:T(8,128)S(1)}, f32[2,32,16,1024]{3,2,1,0:T(8,128)}, u32[]{:S(2)}) copy-start(f32[2,32,16,1024]{3,2,1,0:T(8,128)} %param.6) | copy-start | bytes 12582916
  4.1 16.7 %collective-permute-start.4 = (f32[4,16,1024]{2,0,1:T(4,128)}, f32[4,16,1024]{2,0,1:T(4,128)}, u32[]{:S(2)}, u32[]{:S(2)}) collective-permute-start(f32[4,16,1024]{2,0,1:T(4,128)} %bitcast.95), channel_id=1, source_target_pairs={{0,8},{8,16},{16,24},{1,9},{9,17},{17,25},{2,10},{10,18},{18,26},{... | collective-permute-start | bytes 786440 | tf_op jit(solution)/shard_map/ppermute | solution.py:22
  10.5 22.2 %collective-permute-start.1 = (f32[8,16,1024]{2,0,1:T(8,128)}, f32[8,16,1024]{2,0,1:T(8,128)S(1)}, u32[]{:S(2)}, u32[]{:S(2)}) collective-permute-start(f32[8,16,1024]{2,0,1:T(8,128)} %bitcast.92), channel_id=1, source_target_pairs={{8,0},{16,8},{24,16},{9,1},{17,9},{25,17},{10,2},{18,10},{26,18},{... | collective-permute-start | bytes 1572872 | tf_op jit(solution)/shard_map/ppermute | solution.py:24
  12.9 19.8 %collective-permute-start = (f32[8,16,1024]{2,0,1:T(8,128)}, f32[8,16,1024]{2,0,1:T(8,128)S(1)}, u32[]{:S(2)}, u32[]{:S(2)}) collective-permute-start(f32[8,16,1024]{2,0,1:T(8,128)} %bitcast.93), channel_id=1, source_target_pairs={{0,8},{8,16},{16,24},{1,9},{9,17},{17,25},{2,10},{10,18},{18,26},{... | collective-permute-start | bytes 1572872 | tf_op jit(solution)/shard_map/ppermute | solution.py:22
  17.4 1.9 copy-start.10
  19.2 1.5 copy-start.11
  20.7 1.4 copy-start.4
  24.2 66.0 %collective-permute-start.6 = (f32[40,4,1024]{2,0,1:T(8,128)}, f32[40,4,1024]{2,0,1:T(8,128)}, u32[]{:S(2)}, u32[]{:S(2)}) collective-permute-start(f32[40,4,1024]{2,0,1:T(8,128)} %get-tuple-element.75), channel_id=1, source_target_pairs={{0,1},{1,2},{2,3},{3,4},{4,5},{5,6},{6,7},{8,9},{9,10},{10,11},{11... | collective-permute-start | bytes 1966088 | tf_op jit(solution)/shard_map/ppermute | solution.py:22
  28.5 61.6 %collective-permute-start.7 = (f32[40,4,1024]{2,0,1:T(8,128)}, f32[40,4,1024]{2,0,1:T(8,128)}, u32[]{:S(2)}, u32[]{:S(2)}) collective-permute-start(f32[40,4,1024]{2,0,1:T(8,128)} %get-tuple-element.76), channel_id=1, source_target_pairs={{1,0},{2,1},{3,2},{4,3},{5,4},{6,5},{7,6},{9,8},{10,9},{11,10},{12... | collective-permute-start | bytes 1966088 | tf_op jit(solution)/shard_map/ppermute | solution.py:24
  32.7 1.4 copy-start.2
  34.0 56.2 %copy-start.5 = (f32[1,32,16,1024]{3,1,2,0:T(8,128)S(1)}, f32[1,32,16,1024]{3,1,2,0:T(8,128)}, u32[]{:S(2)}) copy-start(f32[1,32,16,1024]{3,1,2,0:T(8,128)} %copy-done.4) | copy-start | bytes 6291460
  35.5 88.4 %collective-permute-start.2 = (f32[48,8,1024]{2,0,1:T(8,128)}, f32[48,8,1024]{2,0,1:T(8,128)S(1)}, u32[]{:S(2)}, u32[]{:S(2)}) collective-permute-start(f32[48,8,1024]{2,0,1:T(8,128)} %get-tuple-element.73), channel_id=1, source_target_pairs={{0,1},{1,2},{2,3},{3,4},{4,5},{5,6},{6,7},{8,9},{9,10},{10,11},{11... | collective-permute-start | bytes 4718600 | tf_op jit(solution)/shard_map/ppermute | solution.py:22
  40.2 84.9 %collective-permute-start.3 = (f32[48,8,1024]{2,0,1:T(8,128)S(1)}, f32[48,8,1024]{2,0,1:T(8,128)}, u32[]{:S(2)}, u32[]{:S(2)}) collective-permute-start(f32[48,8,1024]{2,0,1:T(8,128)S(1)} %get-tuple-element.74), channel_id=1, source_target_pairs={{1,0},{2,1},{3,2},{4,3},{5,4},{6,5},{7,6},{9,8},{10,9},{11,10},{12... | collective-permute-start | bytes 4718600 | tf_op jit(solution)/shard_map/ppermute | solution.py:24
  99.8 25.3 %copy-start.3 = (f32[1,32,16,1024]{3,1,2,0:T(8,128)S(1)}, f32[1,32,16,1024]{3,1,2,0:T(8,128)}, u32[]{:S(2)}) copy-start(f32[1,32,16,1024]{3,1,2,0:T(8,128)} %copy-done.2) | copy-start | bytes 6291460
  123.9 1.2 copy-start.9
  977.3 9.3 copy-start.6
  984.5 2.1 copy-start.7
  986.6 9.6 copy-start.1
  988.8 1.8 collective-permute-start.8
  991.0 4.4 collective-permute-start.9
where the time goes:
time: 1000 us; the launch traced here: 996 us
  matrix products  553 us (55%)
  local copies, waits for them, and re-layouts  261 us (26%)
  other arithmetic  81.6 us (8%)
  waiting for transfers between devices  76 us (8%)
  starting transfers between devices  23.5 us (2%)
    dot_general x32, matrix products, one_plane(): mixed = jnp.dot(table, hat_weights, precision=lax.Precision.HIGHEST)  549 us
    dynamic_update_slice x32, local copies, waits for them, and re-layouts, shade_cells(): looked = jnp.moveaxis(lax.map(one_plane, level), 1, 0)  197 us
    ppermute x4, waiting for transfers between devices, extended(): lax.ppermute(tail, axis, [(i, (i + 1) % count) for i in range(ends)])  70.8 us
    dynamic_slice x32, local copies, waits for them, and re-layouts, shade_cells(): looked = jnp.moveaxis(lax.map(one_plane, level), 1, 0)  34.9 us
    add x4, other arithmetic, filter_axis(): total + taps[offset] * lax.slice_in_dim(field, offset, offset + count, ax...  29.4 us
  transfers between devices with their start and end apart: 10, of which 4 were waited for; matrix products, arithmetic and copies ran while one was open for 3% of the time, Pallas kernels for 0%

commit v1 on v0

v1 whole, which is shorter than its diff:
```python
import functools

import jax
import jax.numpy as jnp
import ml_dtypes
import numpy as np
from jax import lax
from jax.experimental import pallas as pl
from jax.experimental.pallas import tpu as pltpu
from jax.sharding import Mesh
from jax.sharding import PartitionSpec as P

RAD = 4
LANES = 128
HALO = 8
PER = LANES // (2 * RAD)

offsets = np.arange(-4.0, 5.0)
bell = np.exp(-(offsets**2) / 8.0)
S_TAPS = bell / np.sqrt(np.sum(bell**2))
slope_raw = offsets * bell
D_TAPS = slope_raw / np.sqrt(np.sum(slope_raw**2))


def split_np(matrix):
    hi = matrix.astype(ml_dtypes.bfloat16)
    lo = (matrix - hi.astype(np.float64)).astype(ml_dtypes.bfloat16)
    return hi, lo


def split(value):
    hi = value.astype(jnp.bfloat16)
    return hi, (value - hi.astype(jnp.float32)).astype(jnp.bfloat16)


def mxu(a, b):
    return jnp.dot(a, b, preferred_element_type=jnp.float32)


def band(taps, rows, cols, shift):
    matrix = np.zeros((rows, cols))
    for row in range(rows):
        for k in range(-RAD, RAD + 1):
            if 0 <= row + k + shift < cols:
                matrix[row, row + k + shift] = taps[k + RAD]
    return matrix


def symmetric(block, n):
    t = [float(x) for x in S_TAPS[RAD:]]
    out = t[0] * block[4 : 4 + n]
    for k in range(1, RAD + 1):
        out = out + t[k] * (block[4 - k : 4 - k + n] + block[4 + k : 4 + k + n])
    return out


def slope(block, n):
    t = [float(x) for x in D_TAPS[RAD:]]
    out = t[1] * (block[5 : 5 + n] - block[3 : 3 + n])
    for k in range(2, RAD + 1):
        out = out + t[k] * (block[4 + k : 4 + k + n] - block[4 - k : 4 - k + n])
    return out


def source_kernel(blocks, edges, f_ref, bh_ref, bl_ref, o_ref):
    planes, rows, columns = f_ref.shape[1:]
    step = pl.program_id(0)
    wide = 2 * LANES
    hi, lo = split(f_ref[0].reshape(planes * rows, columns))
    for j in range(columns // wide):
        left, right = max(0, wide * j - LANES), min(columns, wide * (j + 1) + LANES)
        base = left - (wide * j - LANES)
        bh = bh_ref[base : base + right - left]
        bl = bl_ref[base : base + right - left]
        u = mxu(hi[:, left:right], bh) + mxu(lo[:, left:right], bh) + mxu(hi[:, left:right], bl)
        for h in range(2):
            o_ref[2 * j + h, pl.ds(step * planes, planes)] = u[
                :, h * LANES : (h + 1) * LANES
            ].reshape(planes, rows, LANES)
    if edges:
        total = o_ref.shape[1] - edges
        lane = lax.broadcasted_iota(jnp.int32, (rows, LANES), 1)
        zero = jnp.zeros((rows, LANES), jnp.float32)
        for b in range(blocks):
            acc = zero
            for z in range(planes):
                before = o_ref[b - 1, step * planes + z] if b > 0 else zero
                after = o_ref[b + 1, step * planes + z] if b < blocks - 1 else zero
                both = jnp.where(lane >= LANES // 2, before, after)
                moved = pltpu.roll(both, RAD + 2 * RAD * z, 1)
                acc = jnp.where(lane // (2 * RAD) == z, moved, acc)
            o_ref[b, total + step] = acc


def source(fields, which, bh, bl, edges):
    _, slab, rows, columns = fields.shape
    blocks = columns // LANES
    extra = slab // PER if edges else 0
    return pl.pallas_call(
        functools.partial(source_kernel, blocks, extra),
        grid=(slab // PER,),
        in_specs=[
            pl.BlockSpec((1, PER, rows, columns), lambda i: (which, i, 0, 0)),
            pl.BlockSpec((4 * LANES, 2 * LANES), lambda i: (0, 0)),
            pl.BlockSpec((4 * LANES, 2 * LANES), lambda i: (0, 0)),
        ],
        out_specs=pl.BlockSpec((blocks, slab + extra, rows, LANES), lambda i: (0, 0, 0, 0)),
        out_shape=jax.ShapeDtypeStruct((blocks, slab + extra, rows, LANES), jnp.float32),
        compiler_params=pltpu.CompilerParams(vmem_limit_bytes=48 << 20),
        name="columns_filter",
    )(fields, bh, bl)


def gather_rows(groups, slab, extra, r_ref, hl_ref, hr_ref, zin, ein, sems):
    depth = r_ref.shape[0] // groups
    rows = r_ref.shape[2]
    ends = zin.shape[1] - HALO
    copies = []
    parts = [(r_ref, d * groups + g, d, HALO + g * rows, rows) for d in range(depth) for g in range(groups)]
    parts += [(hl_ref, d, d, 0, HALO) for d in range(depth)]
    parts += [(hr_ref, d, d, ends, HALO) for d in range(depth)]
    for ref, block, d, row, count in parts:
        copies.append(
            pltpu.make_async_copy(
                ref.at[block, pl.ds(0, slab)],
                zin.at[pl.ds(RAD + d * slab, slab), pl.ds(row, count)],
                sems.at[len(copies)],
            )
        )
        if extra:
            copies.append(
                pltpu.make_async_copy(
                    ref.at[block, pl.ds(slab, extra)],
                    ein.at[pl.ds(1 + d * extra, extra), pl.ds(row, count)],
                    sems.at[len(copies)],
                )
            )
    for copy in copies:
        copy.start()
    return copies


def plane_smooth(zin, start, count):
    tiles = []
    for row in range(0, zin.shape[1], 8):
        tiles.append(symmetric(zin[pl.ds(start, count + 2 * RAD), row : row + 8, :], count))
    hi, lo = split(jnp.concatenate(tiles, axis=1))
    return jnp.concatenate([hi, lo, hi], axis=1)


def first_kernel(
    groups, slab, extra, r_ref, hl_ref, hr_ref, lhs_ref, yw_ref, zh_ref, zl_ref, pair_ref, pal_ref,
    o_ref, zin, ein, sm, gx, gy, es, sems,
):
    copies = gather_rows(groups, slab, extra, r_ref, hl_ref, hr_ref, zin, ein, sems)
    planes = zin.shape[0] - 2 * RAD
    rows = sm.shape[1]
    wide = zin.shape[1]
    for ref in (zin, sm):
        ref[:RAD] = jnp.zeros((RAD,) + ref.shape[1:], jnp.float32)
        ref[planes + RAD :] = jnp.zeros((RAD,) + ref.shape[1:], jnp.float32)
    ein[0] = jnp.zeros((wide, LANES), jnp.float32)
    ein[ein.shape[0] - 1] = jnp.zeros((wide, LANES), jnp.float32)
    for copy in copies:
        copy.wait()
    step = 8

    for j in range(es.shape[0]):
        hi, lo = split(jnp.concatenate([ein[j], ein[j + 1], ein[j + 2]], axis=1))
        ez = mxu(hi, zh_ref[...]) + mxu(lo, zh_ref[...]) + mxu(hi, zl_ref[...])
        hi, lo = split(ez)
        es[j] = mxu(lhs_ref[:rows], jnp.concatenate([hi, lo, hi], axis=0))

    def smooth_step(t, carry):
        start = pl.multiple_of(t * step, step)
        stack = plane_smooth(zin, start, step)
        for q in range(0, step, 2):
            out = mxu(lhs_ref[...], jnp.concatenate([stack[q], stack[q + 1]], axis=1))
            for h in range(2):
                part = out[:, h * LANES : (h + 1) * LANES]
                sm[RAD + start + q + h] = part[:rows]
                gx[start + q + h] = part[rows:]
        return carry

    lax.fori_loop(0, planes // step, smooth_step, 0)

    halves = pair_ref.shape[0]
    bins = halves * LANES
    factor = 1.5 * (2.0 / planes)

    def shade_step(t, carry):
        start = pl.multiple_of(t * step, step)
        group = es[start // PER]
        moved = []
        for i in range(step):
            shift = (LANES - 2 * RAD * (lax.rem(start, PER) + i)) % LANES
            moved.append(pltpu.roll(group, shift, 1))
        moved = jnp.concatenate(moved, axis=0)
        own = sm[pl.ds(RAD + start, step)].reshape(step * rows, LANES)
        hi, lo = split(jnp.concatenate([own, moved], axis=1))
        out = mxu(hi, yw_ref[...])
        out = out[:, :LANES] + out[:, LANES:] + mxu(lo, yw_ref[:, :LANES])
        gy[...] = out.reshape(step, rows, LANES)
        for row in range(0, rows, 8):
            block = sm[pl.ds(start, step + 2 * RAD), row : row + 8, :]
            grad_z = slope(block, step)
            grad_x = gx[pl.ds(start, step), row : row + 8, :]
            grad_y = gy[:, row : row + 8, :]
            facing = jnp.abs(0.26726 * grad_z + 0.53452 * grad_x + 0.80178 * grad_y)
            square = jnp.maximum(grad_z * grad_z + grad_x * grad_x + grad_y * grad_y, 0.1)
            shade = 0.3 + 0.7 * facing * lax.rsqrt(square)
            half = 0.5 * (bins - 1)
            level = half * jnp.tanh(0.75 * block[RAD : RAD + step]) + half
            index = jnp.minimum(level.astype(jnp.int32), bins - 2)
            fraction = level - index.astype(jnp.float32)
            for i in range(step):
                at = index[i] & (LANES - 1)
                pair = jnp.take_along_axis(
                    jnp.broadcast_to(pair_ref[0], (8, LANES)), at, axis=1, mode="promise_in_bounds"
                )
                for h in range(1, halves):
                    other = jnp.take_along_axis(
                        jnp.broadcast_to(pair_ref[h], (8, LANES)), at, axis=1, mode="promise_in_bounds"
                    )
                    pair = jnp.where(index[i] >= h * LANES, other, pair)
                low, high = pair & (LANES - 1), pair >> 7
                for c in range(4):
                    colours = jnp.broadcast_to(pal_ref[c], (8, LANES))
                    first = jnp.take_along_axis(colours, low, axis=1, mode="promise_in_bounds")
                    second = jnp.take_along_axis(colours, high, axis=1, mode="promise_in_bounds")
                    looked = first + fraction[i] * (second - first)
                    o_ref[c, start + i, row : row + 8, :] = looked * (shade[i] if c < 3 else factor)
        return carry

    lax.fori_loop(0, planes // step, shade_step, 0)


def second_kernel(groups, slab, r_ref, hl_ref, hr_ref, lhs_ref, c_ref, o_ref, zin, sm, sems):
    copies = gather_rows(groups, slab, 0, r_ref, hl_ref, hr_ref, zin, None, sems)
    planes = zin.shape[0] - 2 * RAD
    rows = o_ref.shape[1]
    zin[:RAD] = jnp.zeros((RAD,) + zin.shape[1:], jnp.float32)
    zin[planes + RAD :] = jnp.zeros((RAD,) + zin.shape[1:], jnp.float32)
    for copy in copies:
        copy.wait()
    step = 8

    def march(t, carry):
        start = pl.multiple_of(t * step, step)
        stack = plane_smooth(zin, start, step)
        for q in range(0, step, 2):
            out = mxu(lhs_ref[...], jnp.concatenate([stack[q], stack[q + 1]], axis=1))
            sm[q] = out[:, :LANES]
            sm[q + 1] = out[:, LANES:]
        through, red, green, blue = carry
        for i in range(step):
            sigmoid = 0.5 * jnp.tanh(sm[i]) + 0.5
            passed = through * jnp.exp(-(c_ref[3, start + i] * sigmoid))
            weight = through - passed
            red = red + weight * c_ref[0, start + i]
            green = green + weight * c_ref[1, start + i]
            blue = blue + weight * c_ref[2, start + i]
            through = passed
        return through, red, green, blue

    zero = jnp.zeros((rows, LANES), jnp.float32)
    through, red, green, blue = lax.fori_loop(
        0, planes // step, march, (zero + 1.0, zero, zero, zero)
    )
    for c, value in enumerate((red, green, blue, through)):
        o_ref[c] = value


def vmem_call(kernel, out_shape, scratch, in_specs, name):
    return pl.pallas_call(
        kernel,
        in_specs=in_specs,
        out_specs=pl.BlockSpec(memory_space=pltpu.VMEM),
        out_shape=jax.ShapeDtypeStruct(out_shape, jnp.float32),
        scratch_shapes=scratch,
        compiler_params=pltpu.CompilerParams(vmem_limit_bytes=56 << 20),
        name=name,
    )


def row_halo(blocks, groups, count):
    depth = blocks.shape[0] // groups
    shaped = blocks.reshape((depth, groups) + blocks.shape[1:])
    head = shaped[:, 0, :, :HALO]
    tail = shaped[:, groups - 1, :, shaped.shape[3] - HALO :]
    left = lax.ppermute(tail, "strips", [(i, i + 1) for i in range(count - 1)])
    right = lax.ppermute(head, "strips", [(i + 1, i) for i in range(count - 1)])
    return left, right


def local(depth, count, groups, fields, colour_palette, opacity_palette, tf_index):
    slab, strip, columns = fields.shape[1:]
    extra = slab // PER
    planes = slab * depth
    rows = strip * groups
    wide = rows + 2 * HALO
    bins = tf_index.shape[0]

    bh, bl = split_np(band(S_TAPS, 2 * LANES, 4 * LANES, LANES).T)
    smooth_rows = band(S_TAPS, rows + 2 * RAD, wide, HALO - RAD)
    slope_rows = band(D_TAPS, rows, rows + 2 * RAD, RAD)
    forms = []
    for case in range(4):
        inside = np.ones((rows + 2 * RAD, 1))
        if case & 1:
            inside[:RAD] = 0
        if case & 2:
            inside[-RAD:] = 0
        both = np.concatenate([smooth_rows[RAD:-RAD], slope_rows @ (inside * smooth_rows)], axis=0)
        hi, lo = split_np(both)
        forms.append(np.concatenate([hi, hi, lo], axis=1))
    place = lax.axis_index("strips")
    case = (place == 0).astype(jnp.int32) + 2 * (place == count - 1).astype(jnp.int32)
    lhs = lax.dynamic_index_in_dim(jnp.asarray(np.stack(forms)), case, 0, keepdims=False)
    across = np.zeros((2 * LANES, LANES))
    across[:LANES] = band(D_TAPS, LANES, LANES, 0).T
    for lane in range(LANES):
        for k in range(-RAD, RAD + 1):
            if lane + k < 0:
                across[LANES + lane + k + RAD, lane] = D_TAPS[k + RAD]
            if lane + k >= LANES:
                across[LANES + RAD + lane + k - LANES, lane] = D_TAPS[k + RAD]
    yw = np.concatenate(split_np(across), axis=1)
    zh, zl = split_np(np.kron(band(S_TAPS, PER, 3 * PER, PER).T, np.eye(2 * RAD)))

    following = jnp.concatenate([tf_index[1:], tf_index[-1:]])
    pair = (tf_index + LANES * following).reshape(bins // LANES, 1, LANES)
    palette = jnp.concatenate([colour_palette, opacity_palette[None]], axis=0)
    palette = jnp.pad(palette, ((0, 0), (0, LANES - palette.shape[1])))[:, None, :]

    group_axes = ("depth", "pair")
    sent0 = source(fields, 0, bh, bl, True)
    sent1 = source(fields, 1, bh, bl, False)
    got0 = lax.all_to_all(sent0, group_axes, 0, 0, tiled=True)
    left0, right0 = row_halo(got0, groups, count)
    got1 = lax.all_to_all(sent1, group_axes, 0, 0, tiled=True)
    left1, right1 = row_halo(got1, groups, count)

    anywhere = pl.BlockSpec(memory_space=pl.ANY)
    vmem = pl.BlockSpec(memory_space=pltpu.VMEM)
    f32 = jnp.float32
    parts = depth * (groups + 2)
    coloured = vmem_call(
        functools.partial(first_kernel, groups, slab, extra),
        (4, planes, rows, LANES),
        [
            pltpu.VMEM((planes + 2 * RAD, wide, LANES), f32),
            pltpu.VMEM((planes // PER + 2, wide, LANES), f32),
            pltpu.VMEM((planes + 2 * RAD, rows, LANES), f32),
            pltpu.VMEM((planes, rows, LANES), f32),
            pltpu.VMEM((8, rows, LANES), f32),
            pltpu.VMEM((planes // PER, rows, LANES), f32),
            pltpu.SemaphoreType.DMA((2 * parts,)),
        ],
        [anywhere] * 3 + [vmem] * 6,
        "gradients_and_colours",
    )(got0, left0, right0, lhs, yw, zh, zl, pair, palette)
    image = vmem_call(
        functools.partial(second_kernel, groups, slab),
        (4, rows, LANES),
        [
            pltpu.VMEM((planes + 2 * RAD, wide, LANES), f32),
            pltpu.VMEM((8, rows, LANES), f32),
            pltpu.SemaphoreType.DMA((parts,)),
        ],
        [anywhere] * 3 + [vmem] * 2,
        "march",
    )(got1, left1, right1, lhs[:rows], coloured)
    if groups == 1:
        return image
    return lax.all_to_all(image, "pair", 1, 2, tiled=True)


def solution(mesh):
    depth, tiles = mesh.devices.shape

    def program(fields, colour_palette, opacity_palette, tf_index):
        groups = max(1, fields.shape[3] // (LANES * depth))
        count = tiles // groups
        finer = Mesh(mesh.devices.reshape(depth, count, groups), ("depth", "strips", "pair"))
        return jax.shard_map(
            functools.partial(local, depth, count, groups),
            mesh=finer,
            in_specs=(P(None, "depth", ("strips", "pair"), None), P(), P(), P()),
            out_specs=P(None, ("strips", "pair"), "depth"),
            check_vma=False,
        )(fields, colour_palette, opacity_palette, tf_index)

    return program
```

time: 1000 us -> 165 us (0.17)
  matrix products: 553 us -> 0 us
  local copies, waits for them, and re-layouts: 261 us -> 11.7 us
  other arithmetic: 81.6 us -> 1.77 us
  Pallas kernels: 0 us -> 75.1 us
  waiting for transfers between devices: 76 us -> 49.2 us
    dot_general x36 -> x0, matrix products: 553 us -> none  [the longest x32 549 us: one_plane(): mixed = jnp.dot(table, hat_weights, precision=lax.Precision.HIGHEST)]
    dynamic_update_slice x32 -> x0, local copies, waits for them, and re-layouts: 197 us -> none  [shade_cells(): looked = jnp.moveaxis(lax.map(one_plane, level), 1, 0)]
    pallas_call x0 -> x4, Pallas kernels: none -> 75.1 us  [the longest x1 54.1 us: local(): vmem_call(functools.partial(first_kernel, groups, slab, extra), (4, plane...]
    ppermute x10 -> x4, waiting for transfers between devices: 76 us -> 10.1 us  [the longest x2 5.97 us: row_halo(): left = lax.ppermute(tail, 'strips', [(i, i + 1) for i in range(count - 1)])]
    add x7 -> x1, other arithmetic: 47.3 us -> 1.23 us  [local(): pair = (tf_index + LANES * following).reshape(bins // LANES, 1, LANES)]
    all_to_all x0 -> x2, waiting for transfers between devices: none -> 39.1 us  [the longest x1 20.1 us: local(): got1 = lax.all_to_all(sent1, group_axes, 0, 0, tiled=True)]
    dynamic_slice x35 -> x0, local copies, waits for them, and re-layouts: 35.1 us -> none  [the longest x32 34.9 us: shade_cells(): looked = jnp.moveaxis(lax.map(one_plane, level), 1, 0)]
    ppermute x10 -> x4, starting transfers between devices: 23.5 us -> 10.8 us  [the longest x2 8.18 us: row_halo(): left = lax.ppermute(tail, 'strips', [(i, i + 1) for i in range(count - 1)])]
  transfers between devices with their start and end apart: 10 -> 6, of which waited for: 4 -> 4; matrix products, arithmetic and copies ran while one was open for 3% -> 5% of each run, Pallas kernels for 0% -> 37%
where the time goes in v1:
time: 165 us; the launch traced here: 164 us
  Pallas kernels  75.1 us (46%)
  waiting for transfers between devices  49.2 us (30%)
  starting transfers between devices  19.7 us (12%)
  local copies, waits for them, and re-layouts  11.7 us (7%)
  blocking collectives  6.5 us (4%)
  other arithmetic  1.77 us (1%)
    pallas_call x1, Pallas kernels, local(): vmem_call(functools.partial(first_kernel, groups, slab, extra), (4, plane...  54.1 us
    all_to_all x1, waiting for transfers between devices, local(): got1 = lax.all_to_all(sent1, group_axes, 0, 0, tiled=True)  20.1 us
    all_to_all x1, waiting for transfers between devices, local(): got0 = lax.all_to_all(sent0, group_axes, 0, 0, tiled=True)  19 us
    pallas_call x2, Pallas kernels, source(): pl.pallas_call(functools.partial(source_kernel, blocks, extra), grid=(sla...  10.5 us
    pallas_call x1, Pallas kernels, local(): vmem_call(functools.partial(second_kernel, groups, slab), (4, rows, LANES...  10.5 us
    ppermute x2, starting transfers between devices, row_halo(): left = lax.ppermute(tail, 'strips', [(i, i + 1) for i in range(count - 1)])  8.18 us
    all_to_all x1, blocking collectives, local(): return lax.all_to_all(image, 'pair', 1, 2, tiled=True)  6.5 us
    ppermute x2, waiting for transfers between devices, row_halo(): left = lax.ppermute(tail, 'strips', [(i, i + 1) for i in range(count - 1)])  5.97 us
  transfers between devices with their start and end apart: 6, of which 4 were waited for; matrix products, arithmetic and copies ran while one was open for 5% of the time, Pallas kernels for 37%

profile of v1, /device:TPU:0, one launch (start us, length us, event | category | flops | bytes accessed | tf_op | source)
XLA Modules:
  0.0 164.2 jit_solution(1361425280669143956)
XLA Ops:
  0.0 0.9 copy-done
  1.0 0.9 copy-done.2
  1.9 4.5 %columns_filter.2 = f32[8,32,16,128]{3,2,1,0:T(8,128)} custom-call(f32[2,32,16,1024]{3,2,1,0:T(8,128)} %f_ref.3, bf16[512,256]{1,0:T(8,128)(2,1)S(1)} %copy-done, bf16[512,256]{1,0:T(8,128)(2,1)S(1)} %copy-done.2), custom_call_target="tpu_custom_call" | custom-call | tf_op jit(solution)/shard_map/columns_filter/pallas_call | solution.py:99
  6.4 5.3 %all-to-all-start = ((f32[8,32,16,128]{3,2,1,0:T(8,128)}), f32[8,32,16,128]{3,2,1,0:T(8,128)}, u32[]{:S(2)}, u32[]{:S(2)}) async-start(f32[8,32,16,128]{3,2,1,0:T(8,128)} %columns_filter.2), calls=%async_computation | async-start | bytes 4194304 | tf_op jit(solution)/shard_map/all_to_all | solution.py:341
  11.8 6.0 %columns_filter.3 = f32[8,34,16,128]{3,2,1,0:T(8,128)} custom-call(f32[2,32,16,1024]{3,2,1,0:T(8,128)} %f_ref.3, bf16[512,256]{1,0:T(8,128)(2,1)S(1)} %copy-done.1, bf16[512,256]{1,0:T(8,128)(2,1)S(1)} %copy-done.3), custom_call_target="tpu_custom_call" | custom-call | tf_op jit(solution)/shard_map/columns_filter/pallas_call | solution.py:99
  17.8 20.1 %all-to-all-done.r_ref = f32[8,32,16,128]{3,2,1,0:T(8,128)} async-done(((f32[8,32,16,128]{3,2,1,0:T(8,128)}), f32[8,32,16,128]{3,2,1,0:T(8,128)}, u32[]{:S(2)}, u32[]{:S(2)}) %all-to-all-start) | async-done | bytes 2097184 | tf_op jit(solution)/shard_map/all_to_all | solution.py:341
  37.9 3.6 %all-to-all-start.1 = ((f32[8,34,16,128]{3,2,1,0:T(8,128)}), f32[8,34,16,128]{3,2,1,0:T(8,128)S(1)}, u32[]{:S(2)}, u32[]{:S(2)}) async-start(f32[8,34,16,128]{3,2,1,0:T(8,128)} %columns_filter.3), calls=%async_computation.1 | async-start | bytes 4456448 | tf_op jit(solution)/shard_map/all_to_all | solution.py:339
  41.5 0.0 copy-start.10
  41.5 0.1 slice.30
  41.6 0.6 slice.31
  42.2 2.3 %slice_bitcast_fusion.2 = (f32[4,32,8,128]{3,2,1,0:T(8,128)}, f32[4,32,8,128]{3,2,1,0:T(8,128)}) fusion(f32[4,2,32,16,128]{4,3,2,1,0:T(8,128)} %bitcast), kind=kLoop, calls=%fused_computation.2 | loop fusion | bytes 2097152 | tf_op jit(solution)/shard_map/squeeze | solution.py:289
  44.4 4.1 %collective-permute-start = (f32[4,32,8,128]{3,2,1,0:T(8,128)}, f32[4,32,8,128]{3,2,1,0:T(8,128)S(1)}, u32[]{:S(2)}, u32[]{:S(2)}) collective-permute-start(f32[4,32,8,128]{3,2,1,0:T(8,128)} %get-tuple-element.8), channel_id=1, source_target_pairs={{0,2},{2,4},{4,6},{1,3},{3,5},{5,7},{8,10},{10,12},{12,14},{9,11},... | collective-permute-start | bytes 1572872 | tf_op jit(solution)/shard_map/ppermute | solution.py:291
  48.5 1.3 collective-permute-start.1
  49.8 19.0 %all-to-all-done.1.r_ref = f32[8,34,16,128]{3,2,1,0:T(8,128)S(1)} async-done(((f32[8,34,16,128]{3,2,1,0:T(8,128)}), f32[8,34,16,128]{3,2,1,0:T(8,128)S(1)}, u32[]{:S(2)}, u32[]{:S(2)}) %all-to-all-start.1) | async-done | bytes 2228256 | tf_op jit(solution)/shard_map/all_to_all | solution.py:339
  68.9 0.1 slice_bitcast_fusion
  68.9 4.1 %collective-permute-start.2 = (f32[4,34,8,128]{3,2,1,0:T(8,128)S(1)}, f32[4,34,8,128]{3,2,1,0:T(8,128)S(1)}, u32[]{:S(2)}, u32[]{:S(2)}) collective-permute-start(f32[4,34,8,128]{3,2,1,0:T(8,128)S(1)} %get-tuple-element.6), channel_id=1, source_target_pairs={{0,2},{2,4},{4,6},{1,3},{3,5},{5,7},{8,10},{10,12},{12,14},{9,11},... | collective-permute-start | bytes 1671176 | tf_op jit(solution)/shard_map/ppermute | solution.py:291
  73.0 1.3 collective-permute-start.3
  74.4 0.5 select_maximum_fusion
  74.9 1.3 dynamic-slice_bitcast_fusion.1.lhs_ref
  76.2 1.4 dynamic-slice_bitcast_fusion.lhs_ref
  77.6 1.2 fusion
  78.8 6.0 %collective-permute-done.2.hl_ref = f32[4,34,8,128]{3,2,1,0:T(8,128)S(1)} collective-permute-done((f32[4,34,8,128]{3,2,1,0:T(8,128)S(1)}, f32[4,34,8,128]{3,2,1,0:T(8,128)S(1)}, u32[]{:S(2)}, u32[]{:S(2)}) %collective-permute-start.2) | collective-permute-done | bytes 557088 | tf_op jit(solution)/shard_map/ppermute | solution.py:291
  84.8 4.1 %collective-permute-done.3.hr_ref = f32[4,34,8,128]{3,2,1,0:T(8,128)S(1)} collective-permute-done((f32[4,34,8,128]{3,2,1,0:T(8,128)S(1)}, f32[4,34,8,128]{3,2,1,0:T(8,128)S(1)}, u32[]{:S(2)}, u32[]{:S(2)}) %collective-permute-start.3) | collective-permute-done | bytes 557088 | tf_op jit(solution)/shard_map/ppermute | solution.py:292
  88.9 0.8 copy-done.6
  89.7 54.1 %gradients_and_colours.1.c_ref = f32[4,128,32,128]{3,2,1,0:T(8,128)} custom-call(f32[8,34,16,128]{3,2,1,0:T(8,128)} %copy-done.4, f32[4,34,8,128]{3,2,1,0:T(8,128)} %copy-done.5, f32[4,34,8,128]{3,2,1,0:T(8,128)} %copy-done.6, bf16[64,144]{1,0:T(8,128)(2,1)} %dynamic-slice_bitcast_fusion.lhs_ref, bf16[256,256]{1,0:T(8,128)(2,1)} %constant.37.clone.yw_ref, ...), custom_call_target="tpu_custom_call" | custom-call | tf_op jit(solution)/shard_map/gradients_and_colours/pallas_call | solution.py:348
  143.9 0.8 copy-done.7
  144.7 0.8 copy-done.8
  145.6 10.5 %march.1 = f32[4,32,128]{2,1,0:T(8,128)} custom-call(f32[8,32,16,128]{3,2,1,0:T(8,128)} %all-to-all-done.r_ref, f32[4,32,8,128]{3,2,1,0:T(8,128)} %copy-done.7, f32[4,32,8,128]{3,2,1,0:T(8,128)} %copy-done.8, bf16[32,144]{1,0:T(8,128)(2,1)} %dynamic-slice_bitcast_fusion.1.lhs_ref, f32[4,128,32,128]{3,2,1,0:T(8,128)} %gradients_and_colours.1.c_ref), custom_call_target="tpu_custom_call" | custom-call | tf_op jit(solution)/shard_map/march/pallas_call | solution.py:363
  156.1 0.9 copy.21
  157.0 6.5 %all_to_all.28 = f32[4,32,128]{2,0,1:T(4,128)S(1)} all-to-all(f32[4,32,128]{2,0,1:T(4,128)S(1)} %copy.21), channel_id=1, replica_groups=mesh['depth'=4,'strips'=4,'pair'=2] {'pair'}, dimensions={1} | all-to-all | bytes 131072 | tf_op jit(solution)/shard_map/all_to_all | solution.py:376
  163.5 0.1 copy.22
  163.5 0.7 all_to_all.24
  (20 shorter events, 0.0 us)
Async XLA Ops:
  0.0 0.9 copy-start
  1.0 0.9 copy-start.2
  6.4 5.3 %copy-start.1 = (bf16[512,256]{1,0:T(8,128)(2,1)S(1)}, bf16[512,256]{1,0:T(8,128)(2,1)}, u32[]{:S(2)}) copy-start(bf16[512,256]{1,0:T(8,128)(2,1)} %constant.35.clone.bh_ref) | copy-start | bytes 786436
  6.4 5.3 %copy-start.3 = (bf16[512,256]{1,0:T(8,128)(2,1)S(1)}, bf16[512,256]{1,0:T(8,128)(2,1)}, u32[]{:S(2)}) copy-start(bf16[512,256]{1,0:T(8,128)(2,1)} %constant.36.clone.bl_ref) | copy-start | bytes 786436
  6.4 31.4 %all-to-all-start = ((f32[8,32,16,128]{3,2,1,0:T(8,128)}), f32[8,32,16,128]{3,2,1,0:T(8,128)}, u32[]{:S(2)}, u32[]{:S(2)}) async-start(f32[8,32,16,128]{3,2,1,0:T(8,128)} %columns_filter.2), calls=%async_computation | async-start | bytes 4194304 | tf_op jit(solution)/shard_map/all_to_all | solution.py:341
  17.8 23.7 %copy-start.9 = (s32[256]{0:T(256)S(1)}, s32[256]{0:T(256)}, u32[]{:S(2)}) copy-start(s32[256]{0:T(256)} %param.13) | copy-start | bytes 3076
  37.9 31.0 %all-to-all-start.1 = ((f32[8,34,16,128]{3,2,1,0:T(8,128)}), f32[8,34,16,128]{3,2,1,0:T(8,128)S(1)}, u32[]{:S(2)}, u32[]{:S(2)}) async-start(f32[8,34,16,128]{3,2,1,0:T(8,128)} %columns_filter.3), calls=%async_computation.1 | async-start | bytes 4456448 | tf_op jit(solution)/shard_map/all_to_all | solution.py:339
  41.5 32.9 %copy-start.10 = (f32[3,16]{1,0:T(4,128)S(1)}, f32[3,16]{1,0:T(4,128)}, u32[]{:S(2)}) copy-start(f32[3,16]{1,0:T(4,128)} %param.11) | copy-start | bytes 580
  41.5 32.9 %copy-start.11 = (f32[16]{0:T(128)S(1)}, f32[16]{0:T(128)}, u32[]{:S(2)}) copy-start(f32[16]{0:T(128)} %param.12) | copy-start | bytes 196
  44.4 99.4 %collective-permute-start = (f32[4,32,8,128]{3,2,1,0:T(8,128)}, f32[4,32,8,128]{3,2,1,0:T(8,128)S(1)}, u32[]{:S(2)}, u32[]{:S(2)}) collective-permute-start(f32[4,32,8,128]{3,2,1,0:T(8,128)} %get-tuple-element.8), channel_id=1, source_target_pairs={{0,2},{2,4},{4,6},{1,3},{3,5},{5,7},{8,10},{10,12},{12,14},{9,11},... | collective-permute-start | bytes 1572872 | tf_op jit(solution)/shard_map/ppermute | solution.py:291
  48.5 95.4 %collective-permute-start.1 = (f32[4,32,8,128]{3,2,1,0:T(8,128)}, f32[4,32,8,128]{3,2,1,0:T(8,128)S(1)}, u32[]{:S(2)}, u32[]{:S(2)}) collective-permute-start(f32[4,32,8,128]{3,2,1,0:T(8,128)} %get-tuple-element.7), channel_id=1, source_target_pairs={{2,0},{4,2},{6,4},{3,1},{5,3},{7,5},{10,8},{12,10},{14,12},{11,9},... | collective-permute-start | bytes 1572872 | tf_op jit(solution)/shard_map/ppermute | solution.py:292
  68.9 20.1 %copy-start.4 = (f32[8,34,16,128]{3,2,1,0:T(8,128)}, f32[8,34,16,128]{3,2,1,0:T(8,128)S(1)}, u32[]{:S(2)}) copy-start(f32[8,34,16,128]{3,2,1,0:T(8,128)S(1)} %all-to-all-done.1.r_ref) | copy-start | bytes 6684676
  68.9 15.9 %collective-permute-start.2 = (f32[4,34,8,128]{3,2,1,0:T(8,128)S(1)}, f32[4,34,8,128]{3,2,1,0:T(8,128)S(1)}, u32[]{:S(2)}, u32[]{:S(2)}) collective-permute-start(f32[4,34,8,128]{3,2,1,0:T(8,128)S(1)} %get-tuple-element.6), channel_id=1, source_target_pairs={{0,2},{2,4},{4,6},{1,3},{3,5},{5,7},{8,10},{10,12},{12,14},{9,11},... | collective-permute-start | bytes 1671176 | tf_op jit(solution)/shard_map/ppermute | solution.py:291
  73.0 15.9 %collective-permute-start.3 = (f32[4,34,8,128]{3,2,1,0:T(8,128)S(1)}, f32[4,34,8,128]{3,2,1,0:T(8,128)S(1)}, u32[]{:S(2)}, u32[]{:S(2)}) collective-permute-start(f32[4,34,8,128]{3,2,1,0:T(8,128)S(1)} %get-tuple-element.5), channel_id=1, source_target_pairs={{2,0},{4,2},{6,4},{3,1},{5,3},{7,5},{10,8},{12,10},{14,12},{11,9},... | collective-permute-start | bytes 1671176 | tf_op jit(solution)/shard_map/ppermute | solution.py:292
  84.8 4.2 %copy-start.5 = (f32[4,34,8,128]{3,2,1,0:T(8,128)}, f32[4,34,8,128]{3,2,1,0:T(8,128)S(1)}, u32[]{:S(2)}) copy-start(f32[4,34,8,128]{3,2,1,0:T(8,128)S(1)} %collective-permute-done.2.hl_ref) | copy-start | bytes 1671172
  88.9 0.8 copy-start.6
  143.9 0.8 copy-start.7
  144.7 0.9 copy-start.8
